TPU v7x, 128 devices: a whole 4x4x4 slice. The times are simulated.
128 devices in a mesh: node: 32 (over y_hi, z, x), query: 4 (over y_lo, core).
Axes of the slice: x: 4, y: 4 (y_hi: 2, y_lo: 2; y = y_hi * 2 + y_lo), z: 4, core: 2. Of those that a mesh axis runs over, the one named last changes fastest.
Arguments:
- entity_state: bfloat16 [32768, 2048], P('node', 'query'), may hold values from -6 to 6
- edge_tiles: int32 [512, 3, 512], P('node'), may hold values from 0 to 4095, as said below
- query_head: int32 [64], P('query'), may hold values from 0 to 32767
- query_relation: int32 [64], P('query'), may hold values from 0 to 821
- query_table: float32 [822, 32], replicated, may hold values from -6 to 6
- rel_vectors: float32 [2, 822, 32], replicated, may hold values from -1.8 to 1.8
- mix_weight: float32 [2, 32, 32], replicated, may hold values from -1 to 1
- mix_bias: float32 [2, 32], replicated, may hold values from -3 to 3
- cotangent: bfloat16 [32768, 2048], P('node', 'query'), may hold values from -6 to 6
Outputs:
- final_state: bfloat16 [32768, 2048], P('node', 'query')
- weight_grads: float32 [2, 32, 32], replicated
- bias_grads: float32 [2, 32], replicated
Inputs may be any that keep to these rules, and one draw needn't show every extreme that they name: edge_tiles[t,0,:] lies in 0 to 4095, edge_tiles[t,1,:] in 0 to 63, edge_tiles[t,2,:] in 0 to 821.
All inputs are finite; a program needn't handle non-finite values.
Results may differ from a plain program's by a relative error of at most 0.0056.
Values may be sent and summed in bfloat16 or wider, within the bound.
A program may use at most 192 MiB of HBM per device.

v0:
```python
import jax
import jax.numpy as jnp
from jax import lax
from jax.sharding import PartitionSpec as P

DIM = 32


def with_halo(block, sides, width):
    for axis, dim in sides:
        count = lax.axis_size(axis)
        forward = [(i, i + 1) for i in range(count - 1)]
        forward.append((count - 1, 0))
        backward = [(target, source) for source, target in forward]
        low = lax.ppermute(
            lax.slice_in_dim(block, block.shape[dim] - width, None, axis=dim), axis, forward
        )
        high = lax.ppermute(lax.slice_in_dim(block, 0, width, axis=dim), axis, backward)
        block = jnp.concatenate([low, block, high], axis=dim)
    return block


def from_partner(block, axis, apart):
    count = lax.axis_size(axis)
    route = []
    for low in range(count):
        high = low | 1 << apart
        if high != low and high < count:
            route += [(low, high), (high, low)]
    return lax.ppermute(block, axis, route)


def passed_along(block, axis, distance):
    devices = range(lax.axis_size(axis))
    route = [((i - distance) % len(devices), i) for i in devices]
    return lax.ppermute(block, axis, route)


def silu_slope(values):
    sigma = jax.nn.sigmoid(values)
    return sigma * (1.0 + values * (1.0 - sigma))


def target_onehot(edge_block):
    return (edge_block[:, 1, :][:, None, :] == lax.iota(jnp.int32, 64)[None, :, None]).astype(
        jnp.bfloat16
    )


def contributions(grad_panel, edge_block, dst_onehot, rel_table, slot_base, slot_count):
    tile_count = edge_block.shape[0]
    slot_total = edge_block.shape[2]
    col_count = grad_panel.shape[1]
    per_edge = jnp.einsum(
        "tre,trc->tec",
        dst_onehot,
        grad_panel.reshape(tile_count, 64, col_count),
        preferred_element_type=jnp.float32,
    )
    rel_scales = jnp.take(rel_table, edge_block[:, 2, :], axis=0)
    edge_terms = (
        per_edge.reshape(tile_count, slot_total, col_count // DIM, DIM) * rel_scales[:, :, None, :]
    ).reshape(tile_count * slot_total, col_count)
    segment_ids = edge_block[:, 0, :].reshape(-1) - slot_base
    segment_ids = jnp.where(
        (segment_ids >= 0) & (segment_ids < slot_count), segment_ids, slot_count
    )
    summed = jax.ops.segment_sum(edge_terms, segment_ids, num_segments=slot_count + 1)
    return summed[:slot_count]


def reduce_grads(values):
    return lax.psum((values[0], values[1]), ("node", "query"))


def body(
    entity_state,
    edge_tiles,
    query_head,
    query_relation,
    query_table,
    rel_vectors,
    mix_weight,
    mix_bias,
    cotangent,
):
    highest = lax.Precision.HIGHEST
    row_count = entity_state.shape[0]
    tile_count = edge_tiles.shape[0]
    slot_total = edge_tiles.shape[2]
    query_count = query_head.shape[0]
    col_count = query_count * DIM
    mirror_bit = lax.axis_size("node").bit_length() - 2
    first_row = lax.axis_index("node") * row_count
    entity_ids = first_row + lax.iota(jnp.int32, row_count)
    choose_rel = (
        query_relation[:, None] == lax.iota(jnp.int32, query_table.shape[0])[None, :]
    ).astype(jnp.float32)
    query_vec = jnp.dot(
        choose_rel, query_table, precision=highest, preferred_element_type=jnp.float32
    )
    head_match = (entity_ids[:, None] == query_head[None, :]).astype(jnp.float32)
    boundary = (
        (head_match[:, :, None] * query_vec[None, :, :])
        .reshape(row_count, col_count)
        .astype(jnp.bfloat16)
    )
    own_onehot = target_onehot(edge_tiles)

    def window(state_panel):
        sides = with_halo(state_panel, (("node", 0),), row_count)
        mirror = from_partner(state_panel, "node", mirror_bit)
        return jnp.concatenate([sides, mirror], axis=0)

    def run_layer(state_panel, layer_index):
        extended = window(state_panel)
        gathered = jnp.take(extended, edge_tiles[:, 0, :], axis=0)
        rel_scales = jnp.take(rel_vectors[layer_index], edge_tiles[:, 2, :], axis=0)
        message = (
            gathered.reshape(tile_count, slot_total, query_count, DIM) * rel_scales[:, :, None, :]
        ).astype(jnp.bfloat16)
        message = message.reshape(tile_count, slot_total, col_count)
        summed = jnp.einsum(
            "tre,tec->trc", own_onehot, message, preferred_element_type=jnp.float32
        ).reshape(row_count, col_count)
        mixed_in = boundary.astype(jnp.float32) + summed
        update = (
            jnp.einsum(
                "rqd,de->rqe",
                mixed_in.reshape(row_count, query_count, DIM),
                mix_weight[layer_index],
                precision=highest,
            )
            + mix_bias[layer_index]
        )
        result = (
            state_panel.astype(jnp.float32) + jax.nn.silu(update).reshape(row_count, col_count)
        ).astype(jnp.bfloat16)
        return (mixed_in, update, result)

    mixed_zero, update_zero, state_one = run_layer(entity_state, 0)
    mixed_one, update_one, state_two = run_layer(state_one, 1)
    grad_out = cotangent.astype(jnp.float32)
    grad_update_one = grad_out.reshape(row_count, query_count, DIM) * silu_slope(update_one)
    weight_one = jnp.einsum(
        "rqd,rqe->de",
        mixed_one.reshape(row_count, query_count, DIM),
        grad_update_one,
        precision=highest,
    )
    bias_one = jnp.sum(grad_update_one, axis=(0, 1))
    weight_one, bias_one = reduce_grads((weight_one, bias_one))
    grad_mixed_one = (
        jnp.einsum("rqe,de->rqd", grad_update_one, mix_weight[1], precision=highest)
        .reshape(row_count, col_count)
        .astype(jnp.bfloat16)
    )
    window_terms = contributions(
        grad_mixed_one, edge_tiles, own_onehot, rel_vectors[1], 0, 4 * row_count
    )
    own_terms = window_terms[row_count : 2 * row_count]
    back_right = passed_along(window_terms[:row_count].astype(jnp.bfloat16), "node", -1)
    back_left = passed_along(
        window_terms[2 * row_count : 3 * row_count].astype(jnp.bfloat16), "node", 1
    )
    back_mirror = from_partner(
        window_terms[3 * row_count :].astype(jnp.bfloat16), "node", mirror_bit
    )
    adjoint_sum = (
        own_terms
        + back_right.astype(jnp.float32)
        + back_left.astype(jnp.float32)
        + back_mirror.astype(jnp.float32)
    )
    grad_state_one = grad_out + adjoint_sum
    grad_update_zero = grad_state_one.reshape(row_count, query_count, DIM) * silu_slope(update_zero)
    weight_zero = jnp.einsum(
        "rqd,rqe->de",
        mixed_zero.reshape(row_count, query_count, DIM),
        grad_update_zero,
        precision=highest,
    )
    bias_zero = jnp.sum(grad_update_zero, axis=(0, 1))
    weight_zero, bias_zero = reduce_grads((weight_zero, bias_zero))
    weight_grads = jnp.stack([weight_zero, weight_one])
    bias_grads = jnp.stack([bias_zero, bias_one])
    return (state_two, weight_grads, bias_grads)


def solution(mesh):
    placed = (
        P("node", "query"),
        P("node", None, None),
        P("query"),
        P("query"),
        P(),
        P(),
        P(),
        P(),
        P("node", "query"),
    )
    return jax.shard_map(
        body, mesh=mesh, in_specs=placed, out_specs=(P("node", "query"), P(), P()), check_vma=False
    )
```

profile of v0, /device:TPU:1, one launch (start us, length us, event | category | flops | bytes accessed | tf_op | source)
XLA Modules:
  0.0 584.9 jit_solution(341249885668741540)
XLA Ops:
  0.6 9.5 %collective-permute-start.1 = (bf16[1024,512]{1,0:T(8,128)(2,1)}, bf16[1024,512]{1,0:T(8,128)(2,1)}, u32[]{:S(2)}, u32[]{:S(2)}) collective-permute-start(bf16[1024,512]{1,0:T(8,128)(2,1)} %param.13), channel_id=1, source_target_pairs={{4,0},{8,4},{12,8},{16,12},{20,16},{24,20},{28,24},{32,28},{36,32}... | collective-permute-start | bytes 3145736 | tf_op jit(solution)/shard_map/ppermute | solution.py:18
  13.2 27.8 %gather_fusion.1 = f32[8192,32]{1,0:T(8,128)} fusion(f32[822,32]{1,0:T(8,128)S(1)} %bitcast.102, s32[8192]{0:T(1024)S(1)} %broadcast_clamp_fusion), kind=kCustom, calls=%fused_computation.1.clone | custom fusion | bytes 2129920 | tf_op jit(solution)/shard_map/jit(_take)/gather | solution.py:118
  40.9 27.7 %gather_fusion.3 = f32[8192,32]{1,0:T(8,128)} fusion(f32[822,32]{1,0:T(8,128)S(1)} %bitcast.101, s32[8192]{0:T(1024)S(1)} %broadcast_clamp_fusion), kind=kCustom, calls=%fused_computation.3.clone | custom fusion | bytes 2129920 | tf_op jit(solution)/shard_map/jit(_take)/gather | solution.py:118
  68.7 7.5 %broadcast_select_fusion = (f32[16,512,32]{2,1,0:T(8,128)}, f32[16,512,32]{2,1,0:T(8,128)}) fusion(f32[16,512,32]{2,1,0:T(8,128)} %bitcast.109, pred[16,512]{1,0:T(8,128)(4,1)S(1)} %get-tuple-element.22, f32[16,512,32]{2,1,0:T(8,128)} %bitcast.108), kind=kLoop, calls=%fused_computation.25 | loop fusion | flops 524288 | bytes 4202496 | tf_op jit(solution)/shard_map/jit(_take)/select_n | solution.py:118
  76.4 3.8 copy.59
  80.2 3.6 copy.37
  84.3 2.6 mul.87
  86.9 2.8 copy.27
  92.3 3.6 copy.30
  95.9 3.4 mul.95.clone
  99.3 17.7 %copy.64 = f32[64,8,16,512]{3,1,2,0:T(8,128)} copy(f32[64,8,16,512]{3,2,1,0:T(8,128)S(1)} %bitcast.105) | data formatting | bytes 33554432
  117.1 3.5 pad_maximum_fusion
  120.6 36.5 %gather_fusion = bf16[8192,512]{1,0:T(8,128)(2,1)} fusion(bf16[4096,512]{1,0:T(8,128)(2,1)} %pad_maximum_fusion, s32[8192]{0:T(1024)S(1)} %broadcast_clamp_fusion.1), kind=kCustom, calls=%fused_computation.clone | custom fusion | bytes 16809984 | tf_op jit(solution)/shard_map/jit(_take)/gather | solution.py:117
  157.1 12.4 %copy.28 = bf16[16,512,512]{1,2,0:T(8,128)(2,1)} copy(bf16[16,512,512]{2,1,0:T(8,128)(2,1)} %bitcast.107) | data formatting | bytes 16777216 | tf_op jit(solution)/shard_map/jit(_take)/gather | solution.py:117
  169.5 9.7 %fusion.1 = bf16[16,512,512]{1,2,0:T(8,128)(2,1)} fusion(bf16[16,512,512]{1,2,0:T(8,128)(2,1)} %copy.28, f32[16,512,32]{1,2,0:T(8,128)} %copy.30, pred[16,512]{1,0:T(8,128)(4,1)S(1)} %get-tuple-element.21), kind=kLoop, calls=%fused_computation.8 | loop fusion | flops 16777216 | bytes 17833984 | tf_op jit(solution)/shard_map/convert_element_type | solution.py:121
  179.2 8.0 %convert_add_fusion.3 = (f32[16,64,512]{2,1,0:T(8,128)}, f32[16,64,512]{2,1,0:T(8,128)}) fusion(f32[16,64,512]{2,1,0:T(8,128)S(1)} %copy.27, f32[512]{0:T(512)S(1)} %mul.88, bf16[16,512,512]{1,2,0:T(8,128)(2,1)} %fusion.1, s32[16,512]{1,0:T(8,128)S(1)} %get-tuple-element.20), kind=kOutput, calls=%fused_computation.16 | convolution fusion | flops 539492352 | bytes 14714880 | tf_op jit(solution)/shard_map/tre,tec->trc/dot_general | solution.py:123
  187.2 4.8 copy.32
  192.1 4.9 add.106
  197.0 5.9 %fusion.12 = (f32[1024,16,32]{0,2,1:T(8,128)}, f32[1024,16,32]{0,2,1:T(8,128)}) fusion(f32[32]{0:T(128)S(1)} %get-tuple-element.28, f32[1024,16,32]{0,2,1:T(8,128)} %add.106, f32[2,32,32]{2,1,0:T(8,128)S(1)} %copy-done.15), kind=kOutput, calls=%fused_computation.35 | convolution fusion | flops 203948032 | bytes 6308352 | tf_op jit(solution)/shard_map/rqd,de->rqe/dot_general | solution.py:128
  202.8 2.9 copy.34
  207.9 3.0 collective-permute-start.5
  210.9 7.2 %collective-permute-start.4 = (bf16[1024,512]{1,0:T(8,128)(2,1)S(1)}, bf16[1024,512]{1,0:T(8,128)(2,1)S(1)}, u32[]{:S(2)}, u32[]{:S(2)}) collective-permute-start(bf16[1024,512]{1,0:T(8,128)(2,1)S(1)} %add_convert_fusion.1), channel_id=1, source_target_pairs={{4,0},{8,4},{12,8},{16,12},{20,16},{24,20},{28,24},{32,28},{36,32}... | collective-permute-start | bytes 3145736 | tf_op jit(solution)/shard_map/ppermute | solution.py:18
  218.2 14.8 %collective-permute-done.5 = bf16[1024,512]{1,0:T(8,128)(2,1)S(1)} collective-permute-done((bf16[1024,512]{1,0:T(8,128)(2,1)S(1)}, bf16[1024,512]{1,0:T(8,128)(2,1)S(1)}, u32[]{:S(2)}, u32[]{:S(2)}) %collective-permute-start.5) | collective-permute-done | bytes 1048608 | tf_op jit(solution)/shard_map/ppermute | solution.py:30
  232.9 5.9 %collective-permute-done.4 = bf16[1024,512]{1,0:T(8,128)(2,1)S(1)} collective-permute-done((bf16[1024,512]{1,0:T(8,128)(2,1)S(1)}, bf16[1024,512]{1,0:T(8,128)(2,1)S(1)}, u32[]{:S(2)}, u32[]{:S(2)}) %collective-permute-start.4) | collective-permute-done | bytes 1048608 | tf_op jit(solution)/shard_map/ppermute | solution.py:18
  238.9 7.6 %collective-permute-done.3 = bf16[1024,512]{1,0:T(8,128)(2,1)S(1)} collective-permute-done((bf16[1024,512]{1,0:T(8,128)(2,1)S(1)}, bf16[1024,512]{1,0:T(8,128)(2,1)S(1)}, u32[]{:S(2)}, u32[]{:S(2)}) %collective-permute-start.3) | collective-permute-done | bytes 1048608 | tf_op jit(solution)/shard_map/ppermute | solution.py:15
  248.9 36.5 %gather_fusion.2 = bf16[8192,512]{1,0:T(8,128)(2,1)} fusion(bf16[4096,512]{1,0:T(8,128)(2,1)} %pad_maximum_fusion.1, s32[8192]{0:T(1024)S(1)} %broadcast_clamp_fusion.1), kind=kCustom, calls=%fused_computation.2.clone | custom fusion | bytes 16809984 | tf_op jit(solution)/shard_map/jit(_take)/gather | solution.py:117
  285.4 12.3 %copy.35 = bf16[16,512,512]{1,2,0:T(8,128)(2,1)} copy(bf16[16,512,512]{2,1,0:T(8,128)(2,1)} %bitcast.106) | data formatting | bytes 16777216 | tf_op jit(solution)/shard_map/jit(_take)/gather | solution.py:117
  297.7 9.7 %fusion = bf16[16,512,512]{1,2,0:T(8,128)(2,1)} fusion(bf16[16,512,512]{1,2,0:T(8,128)(2,1)} %copy.35, f32[16,512,32]{1,2,0:T(8,128)} %copy.37, pred[16,512]{1,0:T(8,128)(4,1)S(1)} %get-tuple-element.21), kind=kLoop, calls=%fused_computation.6 | loop fusion | flops 16777216 | bytes 17833984 | tf_op jit(solution)/shard_map/convert_element_type | solution.py:121
  307.4 8.0 %convert_add_fusion.2 = (f32[16,64,512]{2,1,0:T(8,128)}, f32[16,64,512]{2,1,0:T(8,128)}) fusion(f32[16,64,512]{2,1,0:T(8,128)S(1)} %copy.27, f32[512]{0:T(512)S(1)} %mul.88, bf16[16,512,512]{1,2,0:T(8,128)(2,1)} %fusion, s32[16,512]{1,0:T(8,128)S(1)} %get-tuple-element.20), kind=kOutput, calls=%fused_computation.15 | convolution fusion | flops 539492352 | bytes 14714880 | tf_op jit(solution)/shard_map/tre,tec->trc/dot_general | solution.py:123
  315.4 4.8 copy.39
  320.2 3.5 add.113
  323.7 5.8 fusion.37
  334.5 8.2 %fusion.9 = f32[16,512,512]{2,1,0:T(8,128)} fusion(bf16[16,64,512]{1,0,2:T(8,128)(2,1)S(1)} %convert_element_type.93, s32[16,512]{1,0:T(8,128)S(1)} %get-tuple-element.20), kind=kOutput, calls=%fused_computation.23 | convolution fusion | flops 537395200 | bytes 17858560 | tf_op jit(solution)/shard_map/tre,trc->tec/dot_general | solution.py:54
  342.7 17.4 %copy.47 = f32[8192,512]{0,1:T(8,128)} copy(f32[8192,512]{1,0:T(8,128)} %bitcast.104) | data formatting | bytes 33554432 | tf_op jit(solution)/shard_map/reshape | solution.py:62
  360.1 17.8 %mul.105 = f32[8192,512]{0,1:T(8,128)} multiply(f32[8192,512]{0,1:T(8,128)} %copy.47, f32[8192,512]{0,1:T(8,128)} %bitcast.103) | non-fusion elementwise | flops 4194304 | bytes 50331648 | tf_op jit(solution)/shard_map/mul | solution.py:62
  378.0 17.4 %copy.48 = f32[8192,512]{1,0:T(8,128)} copy(f32[8192,512]{0,1:T(8,128)} %mul.105) | data formatting | bytes 33554432 | tf_op jit(solution)/shard_map/mul | solution.py:62
  395.4 52.9 %scatter_custom_fusion = f32[4097,512]{1,0:T(8,128)} fusion(s32[8192]{0:T(1024)S(1)} %bitcast.117, f32[8192,512]{1,0:T(8,128)} %copy.48, f32[]{:T(128)} %constant.12.clone.1), kind=kCustom, calls=%fused_computation.9 | custom fusion | flops 4194304 | bytes 8391168 | tf_op jit(solution)/shard_map/scatter-add | solution.py:68
  448.3 3.9 convert.5
  455.6 3.9 copy.42
  459.6 3.5 reshape.150
  463.1 2.9 copy.41
  466.0 4.8 copy.50
  470.8 5.0 reshape.154
  475.8 3.1 add_convert_fusion
  481.9 4.5 fusion.8
  486.4 2.9 copy.49
  489.3 3.2 fusion.36
  494.5 89.1 %all-reduce = (f32[1,32,32]{2,1,0:T(8,128)S(1)}, f32[1,32,32]{2,1,0:T(8,128)S(1)}, f32[1,32]{1,0:T(1,128)S(1)}, f32[1,32]{1,0:T(1,128)S(1)}) all-reduce(f32[1,32,32]{2,1,0:T(8,128)S(1)} %fusion.15, f32[1,32,32]{2,1,0:T(8,128)S(1)} %fusion.16, f32[1,32]{1,0:T(1,128)S(1)} %bitcast.119, ...), channel_id=1, replica_groups=mesh['node'=32,'query'=4] {'node','query'}, use_global_device_ids=true, to_apply=%region_2.5 | all-reduce | flops 2112 | bytes 16896 | tf_op jit(solution)/shard_map/psum | solution.py:73
  (78 shorter events, 25.5 us)
Async XLA Ops:
  0.6 75.5 %copy-start = (f32[822,32]{0,1:T(8,128)S(1)}, f32[822,32]{0,1:T(8,128)}, u32[]{:S(2)}) copy-start(f32[822,32]{0,1:T(8,128)} %param.17) | copy-start | bytes 315652
  0.6 116.4 %collective-permute-start.1 = (bf16[1024,512]{1,0:T(8,128)(2,1)}, bf16[1024,512]{1,0:T(8,128)(2,1)}, u32[]{:S(2)}, u32[]{:S(2)}) collective-permute-start(bf16[1024,512]{1,0:T(8,128)(2,1)} %param.13), channel_id=1, source_target_pairs={{4,0},{8,4},{12,8},{16,12},{20,16},{24,20},{28,24},{32,28},{36,32}... | collective-permute-start | bytes 3145736 | tf_op jit(solution)/shard_map/ppermute | solution.py:18
  10.1 106.9 %collective-permute-start = (bf16[1024,512]{1,0:T(8,128)(2,1)}, bf16[1024,512]{1,0:T(8,128)(2,1)}, u32[]{:S(2)}, u32[]{:S(2)}) collective-permute-start(bf16[1024,512]{1,0:T(8,128)(2,1)} %param.13), channel_id=1, source_target_pairs={{0,4},{4,8},{8,12},{12,16},{16,20},{20,24},{24,28},{28,32},{32,36}... | collective-permute-start | bytes 3145736 | tf_op jit(solution)/shard_map/ppermute | solution.py:15
  10.1 106.9 %collective-permute-start.2 = (bf16[1024,512]{1,0:T(8,128)(2,1)}, bf16[1024,512]{1,0:T(8,128)(2,1)}, u32[]{:S(2)}, u32[]{:S(2)}) collective-permute-start(bf16[1024,512]{1,0:T(8,128)(2,1)} %param.13), channel_id=1, source_target_pairs={{0,64},{64,0},{4,68},{68,4},{8,72},{72,8},{12,76},{76,12},{16,80},... | collective-permute-start | bytes 3145736 | tf_op jit(solution)/shard_map/ppermute | solution.py:30
  68.7 7.5 %copy-start.17 = (s32[16]{0:T(128)S(1)}, s32[16]{0:T(128)}, u32[]{:S(2)}) copy-start(s32[16]{0:T(128)} %param.16) | copy-start | bytes 196
  76.4 7.4 %copy-start.13 = (f32[16,32]{1,0:T(8,128)}, f32[16,32]{1,0:T(8,128)S(1)}, u32[]{:S(2)}) copy-start(f32[16,32]{1,0:T(8,128)S(1)} %fusion.24) | copy-start | bytes 6148
  80.1 3.7 copy-start.12
  80.2 3.8 copy-start.18
  84.0 2.9 copy-start.10
  99.2 17.8 %copy-start.16 = (f32[2,32]{1,0:T(2,128)S(1)}, f32[2,32]{1,0:T(2,128)}, u32[]{:S(2)}) copy-start(f32[2,32]{1,0:T(2,128)} %param.20) | copy-start | bytes 772
  99.3 17.8 %copy-start.9 = (bf16[1024,512]{1,0:T(8,128)(2,1)S(1)}, bf16[1024,512]{1,0:T(8,128)(2,1)}, u32[]{:S(2)}) copy-start(bf16[1024,512]{1,0:T(8,128)(2,1)} %param.13) | copy-start | bytes 3145732
  192.1 4.9 copy-start.15
  207.9 38.6 %copy-start.2 = (bf16[1024,512]{1,0:T(8,128)(2,1)}, bf16[1024,512]{1,0:T(8,128)(2,1)S(1)}, u32[]{:S(2)}) copy-start(bf16[1024,512]{1,0:T(8,128)(2,1)S(1)} %add_convert_fusion.1) | copy-start | bytes 3145732
  207.9 25.0 %collective-permute-start.5 = (bf16[1024,512]{1,0:T(8,128)(2,1)S(1)}, bf16[1024,512]{1,0:T(8,128)(2,1)S(1)}, u32[]{:S(2)}, u32[]{:S(2)}) collective-permute-start(bf16[1024,512]{1,0:T(8,128)(2,1)S(1)} %add_convert_fusion.1), channel_id=1, source_target_pairs={{0,64},{64,0},{4,68},{68,4},{8,72},{72,8},{12,76},{76,12},{16,80},... | collective-permute-start | bytes 3145736 | tf_op jit(solution)/shard_map/ppermute | solution.py:30
  210.9 27.9 %collective-permute-start.4 = (bf16[1024,512]{1,0:T(8,128)(2,1)S(1)}, bf16[1024,512]{1,0:T(8,128)(2,1)S(1)}, u32[]{:S(2)}, u32[]{:S(2)}) collective-permute-start(bf16[1024,512]{1,0:T(8,128)(2,1)S(1)} %add_convert_fusion.1), channel_id=1, source_target_pairs={{4,0},{8,4},{12,8},{16,12},{20,16},{24,20},{28,24},{32,28},{36,32}... | collective-permute-start | bytes 3145736 | tf_op jit(solution)/shard_map/ppermute | solution.py:18
  218.1 28.4 %collective-permute-start.3 = (bf16[1024,512]{1,0:T(8,128)(2,1)S(1)}, bf16[1024,512]{1,0:T(8,128)(2,1)S(1)}, u32[]{:S(2)}, u32[]{:S(2)}) collective-permute-start(bf16[1024,512]{1,0:T(8,128)(2,1)S(1)} %add_convert_fusion.1), channel_id=1, source_target_pairs={{0,4},{4,8},{8,12},{12,16},{16,20},{20,24},{24,28},{28,32},{32,36}... | collective-permute-start | bytes 3145736 | tf_op jit(solution)/shard_map/ppermute | solution.py:15
  329.5 1.4 copy-start.6
  452.2 3.4 copy-start.5
  454.1 26.9 %collective-permute-start.6 = (bf16[1024,512]{1,0:T(8,128)(2,1)}, bf16[1024,512]{1,0:T(8,128)(2,1)}, u32[]{:S(2)}, u32[]{:S(2)}) collective-permute-start(bf16[1024,512]{1,0:T(8,128)(2,1)} %get-tuple-element.13), channel_id=1, source_target_pairs={{4,0},{8,4},{12,8},{16,12},{20,16},{24,20},{28,24},{32,28},{36,32}... | collective-permute-start | bytes 3145736 | tf_op jit(solution)/shard_map/ppermute | solution.py:36
  454.3 26.6 %collective-permute-start.8 = (bf16[1024,512]{1,0:T(8,128)(2,1)}, bf16[1024,512]{1,0:T(8,128)(2,1)}, u32[]{:S(2)}, u32[]{:S(2)}) collective-permute-start(bf16[1024,512]{1,0:T(8,128)(2,1)} %get-tuple-element.14), channel_id=1, source_target_pairs={{0,64},{64,0},{4,68},{68,4},{8,72},{72,8},{12,76},{76,12},{16,80},... | collective-permute-start | bytes 3145736 | tf_op jit(solution)/shard_map/ppermute | solution.py:30
  454.4 27.5 %collective-permute-start.7 = (bf16[1024,512]{1,0:T(8,128)(2,1)}, bf16[1024,512]{1,0:T(8,128)(2,1)}, u32[]{:S(2)}, u32[]{:S(2)}) collective-permute-start(bf16[1024,512]{1,0:T(8,128)(2,1)} %get-tuple-element.15), channel_id=1, source_target_pairs={{124,0},{0,4},{4,8},{8,12},{12,16},{16,20},{20,24},{24,28},{28,32}... | collective-permute-start | bytes 3145736 | tf_op jit(solution)/shard_map/ppermute | solution.py:36
  470.8 5.0 copy-start.3
  470.8 8.0 %copy-start.11 = (f32[1024,16]{0,1:T(8,128)S(1)}, f32[1024,16]{0,1:T(8,128)}, u32[]{:S(2)}) copy-start(f32[1024,16]{0,1:T(8,128)} %copy-done.10) | copy-start | bytes 196612
  470.8 8.0 %copy-start.14 = (f32[16,32]{1,0:T(8,128)S(1)}, f32[16,32]{1,0:T(8,128)}, u32[]{:S(2)}) copy-start(f32[16,32]{1,0:T(8,128)} %copy-done.13) | copy-start | bytes 6148
  475.8 3.1 copy-start.4
  475.8 3.1 copy-start.7
  478.9 3.0 copy-start.8
  492.4 92.3 %copy-start.1 = (f32[822,32]{0,1:T(8,128)S(1)}, f32[822,32]{0,1:T(8,128)}, u32[]{:S(2)}) copy-start(f32[822,32]{0,1:T(8,128)} %param.17) | copy-start | bytes 315652
where the time goes:
time: 595 us; the launch traced here: 585 us
  local copies, waits for them, and re-layouts  279 us (47%)
  other arithmetic  123 us (21%)
  blocking collectives  89.1 us (15%)
  matrix products  42 us (7%)
  waiting for transfers between devices  29.3 us (5%)
  starting transfers between devices  21.3 us (4%)
    gather x4, local copies, waits for them, and re-layouts, run_layer(): gathered = jnp.take(extended, edge_tiles[:, 0, :], axis=0)  97.8 us
    psum x1, blocking collectives, reduce_grads(): return lax.psum((values[0], values[1]), ('node', 'query'))  89.1 us
    gather x2, local copies, waits for them, and re-layouts, run_layer(): rel_scales = jnp.take(rel_vectors[layer_index], edge_tiles[:, 2, :], axis=0)  55.5 us
    scatter-add x1, other arithmetic, contributions(): jax.ops.segment_sum(edge_terms, segment_ids, num_segments=slot_count + 1)  52.9 us
    unnamed x46, local copies, waits for them, and re-layouts  23.4 us
    convert_element_type x2, other arithmetic, run_layer(): message = (gathered.reshape(tile_count, slot_total, query_count, DIM) * r...  19.4 us
    add x4, local copies, waits for them, and re-layouts, run_layer(): mixed_in = boundary.astype(jnp.float32) + summed  18 us
    mul x1, other arithmetic, contributions(): per_edge.reshape(tile_count, slot_total, col_count // DIM, DIM)  17.8 us
  transfers between devices with their start and end apart: 9, of which 4 were waited for; matrix products, arithmetic and copies ran while one was open for 23% of the time, Pallas kernels for 0%

commit v1 on v0

--- a/solution.py
+++ b/solution.py
@@ -2,6 +2,7 @@
 import jax.numpy as jnp
 from jax import lax
 from jax.sharding import PartitionSpec as P
+from jax.lax import psum
 
 DIM = 32
 
@@ -70,7 +71,11 @@
 
 
 def reduce_grads(values):
-    return lax.psum((values[0], values[1]), ("node", "query"))
+
+    def lay_squares_here(payload, axis_tag, group_axis):
+        return psum(psum(payload, axis_name=axis_tag), axis_name=group_axis)
+
+    return lay_squares_here((values[0], values[1]), "query", "node")
 
 
 def body(

time: 595 us -> 711 us (1.19)
  the two profiles are of different devices: /device:TPU:1 before, /device:TPU:0 now
where the time goes in v1:
time: 711 us; the launch traced here: 701 us
  local copies, waits for them, and re-layouts  279 us (39%)
  blocking collectives  202 us (28%)
  other arithmetic  121 us (17%)
  matrix products  44.4 us (6%)
  waiting for transfers between devices  29.9 us (4%)
  starting transfers between devices  22.8 us (3%)
    psum x2, blocking collectives, lay_squares_here(): return psum(psum(payload, axis_name=axis_tag), axis_name=group_axis)  202 us
    gather x4, local copies, waits for them, and re-layouts, run_layer(): gathered = jnp.take(extended, edge_tiles[:, 0, :], axis=0)  98.1 us
    gather x2, local copies, waits for them, and re-layouts, run_layer(): rel_scales = jnp.take(rel_vectors[layer_index], edge_tiles[:, 2, :], axis=0)  55.8 us
    scatter-add x1, other arithmetic, contributions(): jax.ops.segment_sum(edge_terms, segment_ids, num_segments=slot_count + 1)  52.9 us
    unnamed x44, local copies, waits for them, and re-layouts  23.4 us
    convert_element_type x2, other arithmetic, run_layer(): message = (gathered.reshape(tile_count, slot_total, query_count, DIM) * r...  19.4 us
    add x4, local copies, waits for them, and re-layouts, run_layer(): mixed_in = boundary.astype(jnp.float32) + summed  18 us
    mul x1, other arithmetic, contributions(): per_edge.reshape(tile_count, slot_total, col_count // DIM, DIM)  17.8 us
  transfers between devices with their start and end apart: 9, of which 4 were waited for; matrix products, arithmetic and copies ran while one was open for 19% of the time, Pallas kernels for 0%

profile of v1, /device:TPU:0, one launch (start us, length us, event | category | flops | bytes accessed | tf_op | source)
XLA Modules:
  0.0 700.5 jit_solution(2573235852452395883)
XLA Ops:
  0.6 9.0 %collective-permute-start.1 = (bf16[1024,512]{1,0:T(8,128)(2,1)}, bf16[1024,512]{1,0:T(8,128)(2,1)}, u32[]{:S(2)}, u32[]{:S(2)}) collective-permute-start(bf16[1024,512]{1,0:T(8,128)(2,1)} %param.13), channel_id=1, source_target_pairs={{4,0},{8,4},{12,8},{16,12},{20,16},{24,20},{28,24},{32,28},{36,32}... | collective-permute-start | bytes 3145736 | tf_op jit(solution)/shard_map/ppermute | solution.py:19
  13.0 27.9 %gather_fusion.1 = f32[8192,32]{1,0:T(8,128)} fusion(f32[822,32]{1,0:T(8,128)S(1)} %bitcast.102, s32[8192]{0:T(1024)S(1)} %broadcast_clamp_fusion), kind=kCustom, calls=%fused_computation.1.clone | custom fusion | bytes 2129920 | tf_op jit(solution)/shard_map/jit(_take)/gather | solution.py:123
  40.9 27.9 %gather_fusion.3 = f32[8192,32]{1,0:T(8,128)} fusion(f32[822,32]{1,0:T(8,128)S(1)} %bitcast.101, s32[8192]{0:T(1024)S(1)} %broadcast_clamp_fusion), kind=kCustom, calls=%fused_computation.3.clone | custom fusion | bytes 2129920 | tf_op jit(solution)/shard_map/jit(_take)/gather | solution.py:123
  68.7 7.4 %broadcast_select_fusion = (f32[16,512,32]{2,1,0:T(8,128)}, f32[16,512,32]{2,1,0:T(8,128)}) fusion(f32[16,512,32]{2,1,0:T(8,128)} %bitcast.109, pred[16,512]{1,0:T(8,128)(4,1)S(1)} %get-tuple-element.26, f32[16,512,32]{2,1,0:T(8,128)} %bitcast.108), kind=kLoop, calls=%fused_computation.25 | loop fusion | flops 524288 | bytes 4202496 | tf_op jit(solution)/shard_map/jit(_take)/select_n | solution.py:123
  76.4 3.8 copy.59
  80.2 3.6 copy.37
  86.9 2.8 copy.27
  92.3 3.6 copy.30
  95.9 3.4 mul.95.clone
  99.3 17.7 %copy.64 = f32[64,8,16,512]{3,1,2,0:T(8,128)} copy(f32[64,8,16,512]{3,2,1,0:T(8,128)S(1)} %bitcast.105) | data formatting | bytes 33554432
  117.1 3.5 pad_maximum_fusion
  120.6 36.7 %gather_fusion = bf16[8192,512]{1,0:T(8,128)(2,1)} fusion(bf16[4096,512]{1,0:T(8,128)(2,1)} %pad_maximum_fusion, s32[8192]{0:T(1024)S(1)} %broadcast_clamp_fusion.1), kind=kCustom, calls=%fused_computation.clone | custom fusion | bytes 16809984 | tf_op jit(solution)/shard_map/jit(_take)/gather | solution.py:122
  157.3 12.5 %copy.28 = bf16[16,512,512]{1,2,0:T(8,128)(2,1)} copy(bf16[16,512,512]{2,1,0:T(8,128)(2,1)} %bitcast.107) | data formatting | bytes 16777216 | tf_op jit(solution)/shard_map/jit(_take)/gather | solution.py:122
  169.7 9.7 %fusion.1 = bf16[16,512,512]{1,2,0:T(8,128)(2,1)} fusion(bf16[16,512,512]{1,2,0:T(8,128)(2,1)} %copy.28, f32[16,512,32]{1,2,0:T(8,128)} %copy.30, pred[16,512]{1,0:T(8,128)(4,1)S(1)} %get-tuple-element.25), kind=kLoop, calls=%fused_computation.8 | loop fusion | flops 16777216 | bytes 17833984 | tf_op jit(solution)/shard_map/convert_element_type | solution.py:126
  179.4 8.0 %convert_add_fusion.3 = (f32[16,64,512]{2,1,0:T(8,128)}, f32[16,64,512]{2,1,0:T(8,128)}) fusion(f32[16,64,512]{2,1,0:T(8,128)S(1)} %copy.27, f32[512]{0:T(512)S(1)} %mul.88, bf16[16,512,512]{1,2,0:T(8,128)(2,1)} %fusion.1, s32[16,512]{1,0:T(8,128)S(1)} %get-tuple-element.24), kind=kOutput, calls=%fused_computation.16 | convolution fusion | flops 539492352 | bytes 14714880 | tf_op jit(solution)/shard_map/tre,tec->trc/dot_general | solution.py:128
  187.5 4.8 copy.32
  192.3 4.9 add.114
  197.2 5.9 fusion.12
  203.1 2.9 copy.34
  208.2 3.3 collective-permute-start.5
  211.4 7.7 %collective-permute-start.4 = (bf16[1024,512]{1,0:T(8,128)(2,1)S(1)}, bf16[1024,512]{1,0:T(8,128)(2,1)S(1)}, u32[]{:S(2)}, u32[]{:S(2)}) collective-permute-start(bf16[1024,512]{1,0:T(8,128)(2,1)S(1)} %add_convert_fusion.1), channel_id=1, source_target_pairs={{4,0},{8,4},{12,8},{16,12},{20,16},{24,20},{28,24},{32,28},{36,32}... | collective-permute-start | bytes 3145736 | tf_op jit(solution)/shard_map/ppermute | solution.py:19
  219.2 14.9 %collective-permute-done.5 = bf16[1024,512]{1,0:T(8,128)(2,1)S(1)} collective-permute-done((bf16[1024,512]{1,0:T(8,128)(2,1)S(1)}, bf16[1024,512]{1,0:T(8,128)(2,1)S(1)}, u32[]{:S(2)}, u32[]{:S(2)}) %collective-permute-start.5) | collective-permute-done | bytes 1048608 | tf_op jit(solution)/shard_map/ppermute | solution.py:31
  234.1 6.4 collective-permute-done.4
  240.5 8.0 %collective-permute-done.3 = bf16[1024,512]{1,0:T(8,128)(2,1)S(1)} collective-permute-done((bf16[1024,512]{1,0:T(8,128)(2,1)S(1)}, bf16[1024,512]{1,0:T(8,128)(2,1)S(1)}, u32[]{:S(2)}, u32[]{:S(2)}) %collective-permute-start.3) | collective-permute-done | bytes 1048608 | tf_op jit(solution)/shard_map/ppermute | solution.py:16
  250.9 36.7 %gather_fusion.2 = bf16[8192,512]{1,0:T(8,128)(2,1)} fusion(bf16[4096,512]{1,0:T(8,128)(2,1)} %pad_maximum_fusion.1, s32[8192]{0:T(1024)S(1)} %broadcast_clamp_fusion.1), kind=kCustom, calls=%fused_computation.2.clone | custom fusion | bytes 16809984 | tf_op jit(solution)/shard_map/jit(_take)/gather | solution.py:122
  287.5 12.3 %copy.35 = bf16[16,512,512]{1,2,0:T(8,128)(2,1)} copy(bf16[16,512,512]{2,1,0:T(8,128)(2,1)} %bitcast.106) | data formatting | bytes 16777216 | tf_op jit(solution)/shard_map/jit(_take)/gather | solution.py:122
  299.9 9.7 %fusion = bf16[16,512,512]{1,2,0:T(8,128)(2,1)} fusion(bf16[16,512,512]{1,2,0:T(8,128)(2,1)} %copy.35, f32[16,512,32]{1,2,0:T(8,128)} %copy.37, pred[16,512]{1,0:T(8,128)(4,1)S(1)} %get-tuple-element.25), kind=kLoop, calls=%fused_computation.6 | loop fusion | flops 16777216 | bytes 17833984 | tf_op jit(solution)/shard_map/convert_element_type | solution.py:126
  309.5 8.0 %convert_add_fusion.2 = (f32[16,64,512]{2,1,0:T(8,128)}, f32[16,64,512]{2,1,0:T(8,128)}) fusion(f32[16,64,512]{2,1,0:T(8,128)S(1)} %copy.27, f32[512]{0:T(512)S(1)} %mul.88, bf16[16,512,512]{1,2,0:T(8,128)(2,1)} %fusion, s32[16,512]{1,0:T(8,128)S(1)} %get-tuple-element.24), kind=kOutput, calls=%fused_computation.15 | convolution fusion | flops 539492352 | bytes 14714880 | tf_op jit(solution)/shard_map/tre,tec->trc/dot_general | solution.py:128
  317.5 4.8 copy.39
  322.4 3.5 add.121
  325.9 5.8 fusion.37
  336.7 8.2 %fusion.9 = f32[16,512,512]{2,1,0:T(8,128)} fusion(bf16[16,64,512]{1,0,2:T(8,128)(2,1)S(1)} %convert_element_type.93, s32[16,512]{1,0:T(8,128)S(1)} %get-tuple-element.24), kind=kOutput, calls=%fused_computation.23 | convolution fusion | flops 537395200 | bytes 17858560 | tf_op jit(solution)/shard_map/tre,trc->tec/dot_general | solution.py:55
  344.9 17.4 %copy.47 = f32[8192,512]{0,1:T(8,128)} copy(f32[8192,512]{1,0:T(8,128)} %bitcast.104) | data formatting | bytes 33554432 | tf_op jit(solution)/shard_map/reshape | solution.py:63
  362.3 17.8 %mul.105 = f32[8192,512]{0,1:T(8,128)} multiply(f32[8192,512]{0,1:T(8,128)} %copy.47, f32[8192,512]{0,1:T(8,128)} %bitcast.103) | non-fusion elementwise | flops 4194304 | bytes 50331648 | tf_op jit(solution)/shard_map/mul | solution.py:63
  380.1 17.4 %copy.48 = f32[8192,512]{1,0:T(8,128)} copy(f32[8192,512]{0,1:T(8,128)} %mul.105) | data formatting | bytes 33554432 | tf_op jit(solution)/shard_map/mul | solution.py:63
  397.6 52.9 %scatter_custom_fusion = f32[4097,512]{1,0:T(8,128)} fusion(s32[8192]{0:T(1024)S(1)} %bitcast.117, f32[8192,512]{1,0:T(8,128)} %copy.48, f32[]{:T(128)} %constant.12.clone.1), kind=kCustom, calls=%fused_computation.9 | custom fusion | flops 4194304 | bytes 8391168 | tf_op jit(solution)/shard_map/scatter-add | solution.py:69
  450.5 3.9 convert.5
  458.4 3.9 copy.42
  462.3 3.5 reshape.150
  465.8 3.0 copy.41
  468.8 4.8 copy.50
  473.6 4.9 reshape.154
  478.5 4.4 fusion.15
  484.9 4.5 fusion.8
  489.4 2.9 copy.49
  492.2 3.2 fusion.36
  497.4 10.5 %all-reduce.1 = (f32[32,32]{1,0:T(8,128)S(1)}, f32[32,32]{1,0:T(8,128)S(1)}, f32[32]{0:T(128)S(1)}, f32[32]{0:T(128)S(1)}) all-reduce(f32[32,32]{1,0:T(8,128)S(1)} %fusion.15, f32[32,32]{1,0:T(8,128)S(1)} %fusion.16, f32[32]{0:T(128)S(1)} %get-tuple-element.15, ...), channel_id=1, replica_groups=mesh['node'=32,'query'=4] {'query'}, use_global_device_ids=true, to_apply=%region_3.6 | all-reduce | flops 2112 | bytes 16896 | tf_op jit(solution)/shard_map/psum | solution.py:76
  507.9 191.2 %all-reduce = (f32[1,32,32]{2,1,0:T(8,128)S(1)}, f32[1,32,32]{2,1,0:T(8,128)S(1)}, f32[1,32]{1,0:T(1,128)S(1)}, f32[1,32]{1,0:T(1,128)S(1)}) all-reduce(f32[1,32,32]{2,1,0:T(8,128)S(1)} %bitcast.118, f32[1,32,32]{2,1,0:T(8,128)S(1)} %bitcast.119, f32[1,32]{1,0:T(1,128)S(1)} %bitcast.120, ...), channel_id=1, replica_groups=mesh['node'=32,'query'=4] {'node'}, use_global_device_ids=true, to_apply=%region_4.7 | all-reduce | flops 2112 | bytes 16896 | tf_op jit(solution)/shard_map/psum | solution.py:76
  (77 shorter events, 28.0 us)
Async XLA Ops:
  0.6 75.5 %copy-start = (f32[822,32]{0,1:T(8,128)S(1)}, f32[822,32]{0,1:T(8,128)}, u32[]{:S(2)}) copy-start(f32[822,32]{0,1:T(8,128)} %param.17) | copy-start | bytes 315652
  0.6 116.4 %collective-permute-start.1 = (bf16[1024,512]{1,0:T(8,128)(2,1)}, bf16[1024,512]{1,0:T(8,128)(2,1)}, u32[]{:S(2)}, u32[]{:S(2)}) collective-permute-start(bf16[1024,512]{1,0:T(8,128)(2,1)} %param.13), channel_id=1, source_target_pairs={{4,0},{8,4},{12,8},{16,12},{20,16},{24,20},{28,24},{32,28},{36,32}... | collective-permute-start | bytes 3145736 | tf_op jit(solution)/shard_map/ppermute | solution.py:19
  9.7 107.4 %collective-permute-start = (bf16[1024,512]{1,0:T(8,128)(2,1)}, bf16[1024,512]{1,0:T(8,128)(2,1)}, u32[]{:S(2)}, u32[]{:S(2)}) collective-permute-start(bf16[1024,512]{1,0:T(8,128)(2,1)} %param.13), channel_id=1, source_target_pairs={{0,4},{4,8},{8,12},{12,16},{16,20},{20,24},{24,28},{28,32},{32,36}... | collective-permute-start | bytes 3145736 | tf_op jit(solution)/shard_map/ppermute | solution.py:16
  9.7 107.4 %collective-permute-start.2 = (bf16[1024,512]{1,0:T(8,128)(2,1)}, bf16[1024,512]{1,0:T(8,128)(2,1)}, u32[]{:S(2)}, u32[]{:S(2)}) collective-permute-start(bf16[1024,512]{1,0:T(8,128)(2,1)} %param.13), channel_id=1, source_target_pairs={{0,64},{64,0},{4,68},{68,4},{8,72},{72,8},{12,76},{76,12},{16,80},... | collective-permute-start | bytes 3145736 | tf_op jit(solution)/shard_map/ppermute | solution.py:31
  68.7 7.4 %copy-start.16 = (s32[16]{0:T(128)S(1)}, s32[16]{0:T(128)}, u32[]{:S(2)}) copy-start(s32[16]{0:T(128)} %param.16) | copy-start | bytes 196
  76.4 7.4 %copy-start.12 = (f32[16,32]{1,0:T(8,128)}, f32[16,32]{1,0:T(8,128)S(1)}, u32[]{:S(2)}) copy-start(f32[16,32]{1,0:T(8,128)S(1)} %fusion.24) | copy-start | bytes 6148
  80.2 3.7 copy-start.11
  80.2 3.8 copy-start.17
  84.1 2.9 copy-start.9
  99.3 17.7 %copy-start.15 = (f32[2,32]{1,0:T(2,128)S(1)}, f32[2,32]{1,0:T(2,128)}, u32[]{:S(2)}) copy-start(f32[2,32]{1,0:T(2,128)} %param.20) | copy-start | bytes 772
  99.3 17.8 %copy-start.8 = (bf16[1024,512]{1,0:T(8,128)(2,1)S(1)}, bf16[1024,512]{1,0:T(8,128)(2,1)}, u32[]{:S(2)}) copy-start(bf16[1024,512]{1,0:T(8,128)(2,1)} %param.13) | copy-start | bytes 3145732
  192.3 4.9 copy-start.14
  208.2 40.4 %copy-start.2 = (bf16[1024,512]{1,0:T(8,128)(2,1)}, bf16[1024,512]{1,0:T(8,128)(2,1)S(1)}, u32[]{:S(2)}) copy-start(bf16[1024,512]{1,0:T(8,128)(2,1)S(1)} %add_convert_fusion.1) | copy-start | bytes 3145732
  208.2 25.9 %collective-permute-start.5 = (bf16[1024,512]{1,0:T(8,128)(2,1)S(1)}, bf16[1024,512]{1,0:T(8,128)(2,1)S(1)}, u32[]{:S(2)}, u32[]{:S(2)}) collective-permute-start(bf16[1024,512]{1,0:T(8,128)(2,1)S(1)} %add_convert_fusion.1), channel_id=1, source_target_pairs={{0,64},{64,0},{4,68},{68,4},{8,72},{72,8},{12,76},{76,12},{16,80},... | collective-permute-start | bytes 3145736 | tf_op jit(solution)/shard_map/ppermute | solution.py:31
  211.4 29.1 %collective-permute-start.4 = (bf16[1024,512]{1,0:T(8,128)(2,1)S(1)}, bf16[1024,512]{1,0:T(8,128)(2,1)S(1)}, u32[]{:S(2)}, u32[]{:S(2)}) collective-permute-start(bf16[1024,512]{1,0:T(8,128)(2,1)S(1)} %add_convert_fusion.1), channel_id=1, source_target_pairs={{4,0},{8,4},{12,8},{16,12},{20,16},{24,20},{28,24},{32,28},{36,32}... | collective-permute-start | bytes 3145736 | tf_op jit(solution)/shard_map/ppermute | solution.py:19
  219.2 29.3 %collective-permute-start.3 = (bf16[1024,512]{1,0:T(8,128)(2,1)S(1)}, bf16[1024,512]{1,0:T(8,128)(2,1)S(1)}, u32[]{:S(2)}, u32[]{:S(2)}) collective-permute-start(bf16[1024,512]{1,0:T(8,128)(2,1)S(1)} %add_convert_fusion.1), channel_id=1, source_target_pairs={{0,4},{4,8},{8,12},{12,16},{16,20},{20,24},{24,28},{28,32},{32,36}... | collective-permute-start | bytes 3145736 | tf_op jit(solution)/shard_map/ppermute | solution.py:16
  331.7 1.4 copy-start.5
  454.4 4.0 copy-start.4
  456.0 28.2 %collective-permute-start.6 = (bf16[1024,512]{1,0:T(8,128)(2,1)}, bf16[1024,512]{1,0:T(8,128)(2,1)}, u32[]{:S(2)}, u32[]{:S(2)}) collective-permute-start(bf16[1024,512]{1,0:T(8,128)(2,1)} %get-tuple-element.17), channel_id=1, source_target_pairs={{4,0},{8,4},{12,8},{16,12},{20,16},{24,20},{28,24},{32,28},{36,32}... | collective-permute-start | bytes 3145736 | tf_op jit(solution)/shard_map/ppermute | solution.py:37
  456.3 27.9 %collective-permute-start.8 = (bf16[1024,512]{1,0:T(8,128)(2,1)}, bf16[1024,512]{1,0:T(8,128)(2,1)}, u32[]{:S(2)}, u32[]{:S(2)}) collective-permute-start(bf16[1024,512]{1,0:T(8,128)(2,1)} %get-tuple-element.18), channel_id=1, source_target_pairs={{0,64},{64,0},{4,68},{68,4},{8,72},{72,8},{12,76},{76,12},{16,80},... | collective-permute-start | bytes 3145736 | tf_op jit(solution)/shard_map/ppermute | solution.py:31
  456.7 28.2 %collective-permute-start.7 = (bf16[1024,512]{1,0:T(8,128)(2,1)S(1)}, bf16[1024,512]{1,0:T(8,128)(2,1)}, u32[]{:S(2)}, u32[]{:S(2)}) collective-permute-start(bf16[1024,512]{1,0:T(8,128)(2,1)S(1)} %get-tuple-element.19), channel_id=1, source_target_pairs={{124,0},{0,4},{4,8},{8,12},{12,16},{16,20},{20,24},{24,28},{28,32}... | collective-permute-start | bytes 3145736 | tf_op jit(solution)/shard_map/ppermute | solution.py:37
  473.6 4.9 copy-start.10
  473.6 4.9 copy-start.13
  478.5 4.4 copy-start.3
  478.5 4.4 copy-start.6
  482.9 2.0 copy-start.7
  495.4 204.9 %copy-start.1 = (f32[822,32]{0,1:T(8,128)S(1)}, f32[822,32]{0,1:T(8,128)}, u32[]{:S(2)}) copy-start(f32[822,32]{0,1:T(8,128)} %param.17) | copy-start | bytes 315652
